TPU v7x, 32 devices: a whole 2x2x4 slice. The times are simulated.
32 devices in a mesh: group: 2 (over x), sec: 16 (over z, y, core).
Axes of the slice: x: 2, y: 2, z: 4, core: 2. Of those that a mesh axis runs over, the one named last changes fastest.
Arguments:
- patches: bfloat16 [32, 128, 128, 128], P(('group', 'sec')), parts along dimension 0, may hold values from -24 to 24
- pair_list: int32 [32, 64], P(('group', 'sec')), parts along dimension 0, may hold values from 0 to 127, as said below
- pair_count: int32 [32], P(('group', 'sec')), parts along dimension 0, may hold values from 0 to 64, as said below
- tissue: int32 [32, 128], P(('group', 'sec')), parts along dimension 0, may hold values 0 or 1
Outputs:
- pair_flow: float32 [32, 2, 64], P(('group', 'sec')), parts along dimension 0
- positions: float32 [32, 2, 128], P(('group', 'sec')), parts along dimension 0
There are 2 independent parts, one for each index of `group`. A program takes and returns all parts, laid end to end along the dimension named above; each array names one. Nothing has to cross between parts.
Inputs may be any that keep to these rules, and one draw needn't show every extreme that they name: `pair_list`: the first pair_count[s] entries of row s are distinct patch indices; the other entries are 0. `pair_count`: some section other than the last has exactly 64 live slots; the last section has 0.
All inputs are finite; a program needn't handle non-finite values. No bound on the sum of `tissue` on one device may be relied on, other than what follows from the above.
Results may differ from a plain program's by a relative error of at most 0.0029.
Values may be sent and summed in bfloat16 or wider, within the bound.
A program may use at most 64 MiB of HBM per device.

v0:
```python
import jax
import jax.numpy as jnp
from jax import lax
from jax.sharding import PartitionSpec as P

GR = 8
ITERS = 3


spring_rate = 0.25
step_rate = 0.15


def from_behind(block, axis, distance):
    devices = range(lax.axis_size(axis))
    route = [(i - distance, i) for i in devices if i - distance in devices]
    return lax.ppermute(block, axis, route)


def padded_2(block, sides, width):
    for axis, dim in sides:
        count = lax.axis_size(axis)
        forward = [(i, i + 1) for i in range(count - 1)]
        backward = [(target, source) for source, target in forward]
        low = lax.ppermute(
            lax.slice_in_dim(block, block.shape[dim] - width, None, axis=dim), axis, forward
        )
        high = lax.ppermute(lax.slice_in_dim(block, 0, width, axis=dim), axis, backward)
        block = jnp.concatenate([low, block, high], axis=dim)
    return block


def dft_tables(length):
    index = jnp.arange(length, dtype=jnp.int32)
    product = index[:, None] * index[None, :] % length
    angle_grid = product.astype(jnp.float32) * (2.0 * jnp.pi / length)
    return (jnp.cos(angle_grid).astype(jnp.bfloat16), jnp.sin(angle_grid).astype(jnp.bfloat16))


def right_mul(patch_block, dft_table):
    return jnp.einsum("lxy,yk->lxk", patch_block, dft_table, preferred_element_type=jnp.float32)


def left_mul(dft_table, patch_block):
    return jnp.einsum("kx,lxy->lky", dft_table, patch_block, preferred_element_type=jnp.float32)


def spectrum_pair(patch_block, cosine_table, sine_table):
    with_cos = right_mul(patch_block, cosine_table).astype(jnp.bfloat16)
    with_sin = right_mul(patch_block, sine_table).astype(jnp.bfloat16)
    real_part = (left_mul(cosine_table, with_cos) - left_mul(sine_table, with_sin)).astype(
        jnp.bfloat16
    )
    imag_part = (-(left_mul(cosine_table, with_sin) + left_mul(sine_table, with_cos))).astype(
        jnp.bfloat16
    )
    return (real_part.astype(jnp.float32), imag_part.astype(jnp.float32))


def soft_peak(lower_block, upper_block, cosine_table, sine_table):
    lower_real, lower_imag = spectrum_pair(lower_block, cosine_table, sine_table)
    upper_real, upper_imag = spectrum_pair(upper_block, cosine_table, sine_table)
    cross_real = (lower_real * upper_real + lower_imag * upper_imag).astype(jnp.bfloat16)
    cross_imag = (lower_real * upper_imag - lower_imag * upper_real).astype(jnp.bfloat16)
    inner_real = (right_mul(cross_real, cosine_table) - right_mul(cross_imag, sine_table)).astype(
        jnp.bfloat16
    )
    inner_imag = (right_mul(cross_real, sine_table) + right_mul(cross_imag, cosine_table)).astype(
        jnp.bfloat16
    )
    raw_corr = left_mul(cosine_table, inner_real) - left_mul(sine_table, inner_imag)
    side_length = raw_corr.shape[-1]
    scores = raw_corr * (64.0 / float(side_length * side_length * side_length * side_length))
    weights = jax.nn.softmax(scores.reshape(raw_corr.shape[0], -1), axis=-1).reshape(raw_corr.shape)
    lag_values = (
        (jnp.arange(side_length) + side_length // 2) % side_length - side_length // 2
    ).astype(jnp.float32)
    shift_rows = jnp.sum(jnp.sum(weights, axis=2) * lag_values[None, :], axis=1)
    shift_cols = jnp.sum(jnp.sum(weights, axis=1) * lag_values[None, :], axis=1)
    return jnp.stack([shift_rows, shift_cols])


def pad_axis(values, before, after, axis_pos):
    widths = [(0, 0)] * values.ndim
    widths[axis_pos % values.ndim] = (before, after)
    return jnp.pad(values, widths)


def plane_force(field_vals, stiffness, grid_rows):
    full_shape = field_vals.shape
    grid_cols = full_shape[-1] // grid_rows
    grid = field_vals.reshape(full_shape[:-1] + (grid_rows, grid_cols))
    stiff_grid = stiffness.reshape(stiffness.shape[:-1] + (1, grid_rows, grid_cols))
    along_cols = (
        0.5 * (stiff_grid[..., 1:] + stiff_grid[..., :-1]) * (grid[..., 1:] - grid[..., :-1])
    )
    col_force = pad_axis(along_cols, 1, 0, -1) - pad_axis(along_cols, 0, 1, -1)
    along_rows = (
        0.5
        * (stiff_grid[..., 1:, :] + stiff_grid[..., :-1, :])
        * (grid[..., 1:, :] - grid[..., :-1, :])
    )
    row_force = pad_axis(along_rows, 1, 0, -2) - pad_axis(along_rows, 0, 1, -2)
    return (col_force + row_force).reshape(full_shape)


def mesh_force(middle, upper, lower, here_field, below_field, stiffness, grid_rows):
    gap_here = upper - middle - here_field[..., 0:2, :]
    gap_below = middle - lower - below_field[..., 0:2, :]
    return (
        plane_force(middle, stiffness, grid_rows)
        - here_field[..., 2:3, :] * gap_here
        + below_field[..., 2:3, :] * gap_below
    )


def on_device(patches, pair_list, pair_count, tissue):
    cosine_table, sine_table = dft_tables(patches.shape[-1])
    own_patches = patches[0]
    listing = pair_list[0]
    live_count = pair_count[0]
    slot_total = listing.shape[0]
    patch_total = own_patches.shape[0]
    lower_list = from_behind(pair_list, "sec", 1)
    picked = own_patches[lower_list[0]]
    upper_block = from_behind(picked[None], "sec", -1)[0]
    lower_block = own_patches[listing]
    valid_mask = (jnp.arange(slot_total) < live_count).astype(jnp.float32)
    slot_flows = soft_peak(lower_block, upper_block, cosine_table, sine_table) * valid_mask[None, :]
    onehot = (listing[:, None] == jnp.arange(patch_total)[None, :]).astype(
        jnp.float32
    ) * valid_mask[:, None]
    moved_flows = jnp.dot(slot_flows, onehot, precision=lax.Precision.HIGHEST)
    pair_field = jnp.concatenate([moved_flows, jnp.sum(onehot, axis=0)[None, :]], axis=0)[None]
    stiffness = spring_rate * (1.0 + 2.0 * tissue.astype(jnp.float32))
    below_field = from_behind(pair_field, "sec", 1)
    positions = jnp.zeros((1, 2, patch_total), jnp.float32)
    for sweep_step in range(ITERS):
        padded = padded_2(positions, (("sec", 0),), 1)
        force_now = mesh_force(
            padded[1:2], padded[2:3], padded[0:1], pair_field, below_field, stiffness, GR
        )
        positions = positions - step_rate * force_now
    return (slot_flows[None], positions)


def solution(mesh):
    return jax.shard_map(
        on_device,
        mesh=mesh,
        in_specs=(
            P(("group", "sec"), None, None, None),
            P(("group", "sec"), None),
            P(("group", "sec")),
            P(("group", "sec"), None),
        ),
        out_specs=(P(("group", "sec"), None, None), P(("group", "sec"), None, None)),
        check_vma=False,
    )
```

profile of v0, /device:TPU:24, one launch (start us, length us, event | category | flops | bytes accessed | tf_op | source)
XLA Modules:
  0.0 98.9 jit_solution(11161900901269148109)
XLA Ops:
  0.6 2.8 %collective-permute-start.2 = (f32[1,2,128]{2,1,0:T(2,128)S(1)}, f32[1,2,128]{2,1,0:T(2,128)S(1)}, u32[]{:S(2)}, u32[]{:S(2)}) collective-permute-start(f32[1,2,128]{2,1,0:T(2,128)S(1)} %broadcast_in_dim.9), channel_id=1, source_target_pairs={{1,0},{2,1},{3,2},{4,3},{5,4},{6,5},{7,6},{8,7},{9,8},{10,9},{11,1... | collective-permute-start | bytes 3080 | tf_op jit(solution)/shard_map/ppermute | solution.py:28
  3.4 1.9 %collective-permute-start.4 = (f32[1,2,128]{2,1,0:T(2,128)S(1)}, f32[1,2,128]{2,1,0:T(2,128)S(1)}, u32[]{:S(2)}, u32[]{:S(2)}) collective-permute-start(f32[1,2,128]{2,1,0:T(2,128)S(1)} %broadcast_in_dim.9), channel_id=1, source_target_pairs={{0,1},{1,2},{2,3},{3,4},{4,5},{5,6},{6,7},{7,8},{8,9},{9,10},{10,1... | collective-permute-start | bytes 3080 | tf_op jit(solution)/shard_map/ppermute | solution.py:25
  5.3 2.7 %collective-permute-start = (s32[1,64]{1,0:T(1,128)}, s32[1,64]{1,0:T(1,128)S(1)}, u32[]{:S(2)}, u32[]{:S(2)}) collective-permute-start(s32[1,64]{1,0:T(1,128)} %param.5), channel_id=1, source_target_pairs={{0,1},{1,2},{2,3},{3,4},{4,5},{5,6},{6,7},{7,8},{8,9},{9,10},{10,1... | collective-permute-start | bytes 776 | tf_op jit(solution)/shard_map/ppermute | solution.py:17
  8.0 0.7 fusion.67
  8.7 0.7 multiply_reduce_fusion.2
  9.4 0.1 reshape.196
  9.6 1.6 %collective-permute-done = s32[1,64]{1,0:T(1,128)S(1)} collective-permute-done((s32[1,64]{1,0:T(1,128)}, s32[1,64]{1,0:T(1,128)S(1)}, u32[]{:S(2)}, u32[]{:S(2)}) %collective-permute-start) | collective-permute-done | bytes 288 | tf_op jit(solution)/shard_map/ppermute | solution.py:17
  11.3 4.4 %gather_fusion.1 = bf16[64,128,128]{2,1,0:T(8,128)(2,1)} fusion(bf16[128,128,128]{2,1,0:T(8,128)(2,1)} %bitcast.93, s32[1024]{0:T(1024)S(1)} %pad_clamp_fusion), kind=kCustom, calls=%fused_computation.1 | custom fusion | bytes 4194560 | tf_op jit(solution)/shard_map/gather | solution.py:125
  15.6 2.2 %collective-permute-start.1 = (bf16[1,64,128,128]{3,2,1,0:T(8,128)(2,1)}, bf16[1,64,128,128]{3,2,1,0:T(8,128)(2,1)}, u32[]{:S(2)}, u32[]{:S(2)}) collective-permute-start(bf16[1,64,128,128]{3,2,1,0:T(8,128)(2,1)} %bitcast.7), channel_id=1, source_target_pairs={{1,0},{2,1},{3,2},{4,3},{5,4},{6,5},{7,6},{8,7},{9,8},{10,9},{11,1... | collective-permute-start | bytes 6291464 | tf_op jit(solution)/shard_map/ppermute | solution.py:17
  17.8 3.1 %gather_fusion = bf16[64,128,128]{2,1,0:T(8,128)(2,1)S(1)} fusion(bf16[128,128,128]{2,1,0:T(8,128)(2,1)} %bitcast.94, s32[1024]{0:T(1024)S(1)} %pad_clamp_fusion.1), kind=kCustom, calls=%fused_computation | custom fusion | bytes 4194560 | tf_op jit(solution)/shard_map/gather | solution.py:127
  21.6 0.1 reshape.197
  21.7 0.1 select_reduce_fusion
  21.8 0.9 convolution_convert_fusion
  22.8 0.9 convolution_convert_fusion.1
  23.7 0.9 fusion.47
  24.7 1.0 fusion.52
  25.6 1.0 negate_convert_fusion.1
  26.6 15.1 %collective-permute-done.1 = bf16[1,64,128,128]{3,2,1,0:T(8,128)(2,1)} collective-permute-done((bf16[1,64,128,128]{3,2,1,0:T(8,128)(2,1)}, bf16[1,64,128,128]{3,2,1,0:T(8,128)(2,1)}, u32[]{:S(2)}, u32[]{:S(2)}) %collective-permute-start.1) | collective-permute-done | bytes 2097184 | tf_op jit(solution)/shard_map/ppermute | solution.py:17
  41.6 2.5 %fusion.15 = bf16[64,128,128]{2,1,0:T(8,128)(2,1)S(1)} fusion(bf16[1,64,128,128]{3,2,1,0:T(8,128)(2,1)} %collective-permute-done.1), kind=kOutput, calls=%fused_computation.27 | convolution fusion | flops 269729792 | bytes 4194304 | tf_op jit(solution)/shard_map/lxy,yk->lxk/dot_general | solution.py:41
  44.2 1.0 fusion.45
  45.1 2.5 %fusion.12 = bf16[64,128,128]{2,1,0:T(8,128)(2,1)S(1)} fusion(bf16[1,64,128,128]{3,2,1,0:T(8,128)(2,1)} %collective-permute-done.1), kind=kOutput, calls=%fused_computation.26 | convolution fusion | flops 269729792 | bytes 4194304 | tf_op jit(solution)/shard_map/lxy,yk->lxk/dot_general | solution.py:41
  47.7 1.0 fusion.49
  48.6 1.0 %negate_convert_fusion = bf16[64,128,128]{2,1,0:T(8,128)(2,1)S(1)} fusion(f32[64,128,128]{2,1,0:T(8,128)S(1)} %fusion.45, bf16[64,128,128]{2,1,0:T(8,128)(2,1)S(1)} %fusion.12), kind=kOutput, calls=%fused_computation.14 | convolution fusion | flops 271826944 | bytes 8388608 | tf_op jit(solution)/shard_map/kx,lxy->lky/dot_general | solution.py:45
  49.6 1.0 %subtract_convert_fusion.1 = bf16[64,128,128]{2,1,0:T(8,128)(2,1)S(1)} fusion(f32[64,128,128]{2,1,0:T(8,128)S(1)} %fusion.49, bf16[64,128,128]{2,1,0:T(8,128)(2,1)S(1)} %fusion.15), kind=kOutput, calls=%fused_computation.16 | convolution fusion | flops 270778368 | bytes 8388608 | tf_op jit(solution)/shard_map/kx,lxy->lky/dot_general | solution.py:45
  50.7 2.2 %fusion.6 = (bf16[64,128,128]{1,2,0:T(8,128)(2,1)S(1)}, bf16[64,128,128]{1,2,0:T(8,128)(2,1)S(1)}) fusion(bf16[64,128,128]{2,1,0:T(8,128)(2,1)S(1)} %subtract_convert_fusion.1, bf16[64,128,128]{2,1,0:T(8,128)(2,1)S(1)} %negate_convert_fusion.1, bf16[64,128,128]{2,1,0:T(8,128)(2,1)S(1)} %negate_convert_fusion, f32[64,128,128]{2,1,0:T(8,128)S(1)} %fusion.52, ...), kind=kOutput, calls=%fused_computation.20 | convolution fusion | flops 283361280 | bytes 16777216 | tf_op jit(solution)/shard_map/kx,lxy->lky/dot_general | solution.py:45
  52.9 2.9 %fusion.43 = f32[64,128,128]{1,2,0:T(8,128)} fusion(bf16[64,128,128]{1,2,0:T(8,128)(2,1)S(1)} %get-tuple-element.11), kind=kOutput, calls=%fused_computation.51 | convolution fusion | flops 268681216 | bytes 6291456 | tf_op jit(solution)/shard_map/lxy,yk->lxk/dot_general | solution.py:41
  55.8 2.9 %fusion.30 = f32[64,128,128]{1,2,0:T(8,128)} fusion(bf16[64,128,128]{1,2,0:T(8,128)(2,1)S(1)} %get-tuple-element.11), kind=kOutput, calls=%fused_computation.50 | convolution fusion | flops 268681216 | bytes 6291456 | tf_op jit(solution)/shard_map/lxy,yk->lxk/dot_general | solution.py:41
  58.8 5.7 %fusion.18 = f32[64,128,128]{2,1,0:T(8,128)} fusion(f32[64,128,128]{1,2,0:T(8,128)} %fusion.43, bf16[64,128,128]{1,2,0:T(8,128)(2,1)S(1)} %get-tuple-element.10), kind=kOutput, calls=%fused_computation.30 | convolution fusion | flops 539459584 | bytes 10485760 | tf_op jit(solution)/shard_map/kx,lxy->lky/dot_general | solution.py:45
  64.5 7.0 %fusion.145 = (f32[64]{0:T(128)S(1)}, f32[64,128,128]{2,1,0:T(8,128)}) fusion(f32[64,128,128]{2,1,0:T(8,128)} %fusion.18, f32[64,128,128]{1,2,0:T(8,128)} %fusion.30, bf16[64,128,128]{1,2,0:T(8,128)(2,1)S(1)} %get-tuple-element.10), kind=kOutput, calls=%fused_computation.166 | convolution fusion | flops 542605248 | bytes 14680320 | tf_op jit(solution)/shard_map/kx,lxy->lky/dot_general | solution.py:45
  71.4 3.3 %fusion.4 = f32[64]{0:T(128)S(1)} fusion(f32[64,128,128]{2,1,0:T(8,128)} %get-tuple-element.13, f32[64]{0:T(128)S(1)} %get-tuple-element.12), kind=kLoop, calls=%fused_computation.18 | loop fusion | flops 2097088 | bytes 4194816 | tf_op jit(solution)/shard_map/reduce_sum | solution.py:74
  74.8 0.1 copy-done
  74.9 1.3 %fusion.144 = (f32[64,128]{1,0:T(8,128)S(1)}, f32[64,128]{1,0:T(8,128)S(1)}) fusion(f32[64]{0:T(128)S(1)} %fusion.4, f32[64,128,128]{2,1,0:T(8,128)S(1)} %copy-done, f32[64]{0:T(128)S(1)} %get-tuple-element.12), kind=kLoop, calls=%fused_computation.165 | loop fusion | flops 4177920 | bytes 4260352 | tf_op jit(solution)/shard_map/reduce_sum | solution.py:78
  76.2 0.1 multiply_reduce_fusion.1
  76.4 0.2 fusion.25
  76.6 2.5 %collective-permute-start.3 = (f32[1,3,128]{2,1,0:T(4,128)S(1)}, f32[1,3,128]{2,1,0:T(4,128)S(1)}, u32[]{:S(2)}, u32[]{:S(2)}) collective-permute-start(f32[1,3,128]{2,1,0:T(4,128)S(1)} %maximum_bitcast_fusion), channel_id=1, source_target_pairs={{0,1},{1,2},{2,3},{3,4},{4,5},{5,6},{6,7},{7,8},{8,9},{9,10},{10,1... | collective-permute-start | bytes 4616 | tf_op jit(solution)/shard_map/ppermute | solution.py:17
  79.1 0.6 maximum_multiply_fusion
  79.6 2.9 %collective-permute-done.3 = f32[1,3,128]{2,1,0:T(4,128)S(1)} collective-permute-done((f32[1,3,128]{2,1,0:T(4,128)S(1)}, f32[1,3,128]{2,1,0:T(4,128)S(1)}, u32[]{:S(2)}, u32[]{:S(2)}) %collective-permute-start.3) | collective-permute-done | bytes 1568 | tf_op jit(solution)/shard_map/ppermute | solution.py:17
  82.7 1.9 %collective-permute-start.5 = (f32[1,2,128]{2,1,0:T(2,128)S(1)}, f32[1,2,128]{2,1,0:T(2,128)S(1)}, u32[]{:S(2)}, u32[]{:S(2)}) collective-permute-start(f32[1,2,128]{2,1,0:T(2,128)S(1)} %multiply_subtract_fusion.2), channel_id=1, source_target_pairs={{1,0},{2,1},{3,2},{4,3},{5,4},{6,5},{7,6},{8,7},{9,8},{10,9},{11,1... | collective-permute-start | bytes 3080 | tf_op jit(solution)/shard_map/ppermute | solution.py:28
  84.6 2.4 %collective-permute-start.6 = (f32[1,2,128]{2,1,0:T(2,128)S(1)}, f32[1,2,128]{2,1,0:T(2,128)S(1)}, u32[]{:S(2)}, u32[]{:S(2)}) collective-permute-start(f32[1,2,128]{2,1,0:T(2,128)S(1)} %multiply_subtract_fusion.2), channel_id=1, source_target_pairs={{0,1},{1,2},{2,3},{3,4},{4,5},{5,6},{6,7},{7,8},{8,9},{9,10},{10,1... | collective-permute-start | bytes 3080 | tf_op jit(solution)/shard_map/ppermute | solution.py:25
  87.1 0.1 subtract_add_fusion.1
  87.2 0.1 reshape.199
  87.3 3.1 %collective-permute-done.6 = f32[1,2,128]{2,1,0:T(2,128)S(1)} collective-permute-done((f32[1,2,128]{2,1,0:T(2,128)S(1)}, f32[1,2,128]{2,1,0:T(2,128)S(1)}, u32[]{:S(2)}, u32[]{:S(2)}) %collective-permute-start.6) | collective-permute-done | bytes 1056 | tf_op jit(solution)/shard_map/ppermute | solution.py:25
  90.4 0.1 reshape.200
  90.6 1.9 %collective-permute-start.7 = (f32[1,2,128]{2,1,0:T(2,128)S(1)}, f32[1,2,128]{2,1,0:T(2,128)S(1)}, u32[]{:S(2)}, u32[]{:S(2)}) collective-permute-start(f32[1,2,128]{2,1,0:T(2,128)S(1)} %multiply_subtract_fusion.1), channel_id=1, source_target_pairs={{1,0},{2,1},{3,2},{4,3},{5,4},{6,5},{7,6},{8,7},{9,8},{10,9},{11,1... | collective-permute-start | bytes 3080 | tf_op jit(solution)/shard_map/ppermute | solution.py:28
  92.5 2.4 %collective-permute-start.8 = (f32[1,2,128]{2,1,0:T(2,128)S(1)}, f32[1,2,128]{2,1,0:T(2,128)S(1)}, u32[]{:S(2)}, u32[]{:S(2)}) collective-permute-start(f32[1,2,128]{2,1,0:T(2,128)S(1)} %multiply_subtract_fusion.1), channel_id=1, source_target_pairs={{0,1},{1,2},{2,3},{3,4},{4,5},{5,6},{6,7},{7,8},{8,9},{9,10},{10,1... | collective-permute-start | bytes 3080 | tf_op jit(solution)/shard_map/ppermute | solution.py:25
  95.0 0.1 reshape.201
  95.1 3.2 %collective-permute-done.8 = f32[1,2,128]{2,1,0:T(2,128)S(1)} collective-permute-done((f32[1,2,128]{2,1,0:T(2,128)S(1)}, f32[1,2,128]{2,1,0:T(2,128)S(1)}, u32[]{:S(2)}, u32[]{:S(2)}) %collective-permute-start.8) | collective-permute-done | bytes 1056 | tf_op jit(solution)/shard_map/ppermute | solution.py:25
  98.3 0.6 multiply_subtract_fusion
  (29 shorter events, 0.6 us)
Async XLA Ops:
  0.6 81.9 %collective-permute-start.2 = (f32[1,2,128]{2,1,0:T(2,128)S(1)}, f32[1,2,128]{2,1,0:T(2,128)S(1)}, u32[]{:S(2)}, u32[]{:S(2)}) collective-permute-start(f32[1,2,128]{2,1,0:T(2,128)S(1)} %broadcast_in_dim.9), channel_id=1, source_target_pairs={{1,0},{2,1},{3,2},{4,3},{5,4},{6,5},{7,6},{8,7},{9,8},{10,9},{11,1... | collective-permute-start | bytes 3080 | tf_op jit(solution)/shard_map/ppermute | solution.py:28
  3.4 79.2 %collective-permute-start.4 = (f32[1,2,128]{2,1,0:T(2,128)S(1)}, f32[1,2,128]{2,1,0:T(2,128)S(1)}, u32[]{:S(2)}, u32[]{:S(2)}) collective-permute-start(f32[1,2,128]{2,1,0:T(2,128)S(1)} %broadcast_in_dim.9), channel_id=1, source_target_pairs={{0,1},{1,2},{2,3},{3,4},{4,5},{5,6},{6,7},{7,8},{8,9},{9,10},{10,1... | collective-permute-start | bytes 3080 | tf_op jit(solution)/shard_map/ppermute | solution.py:25
  5.3 5.9 %collective-permute-start = (s32[1,64]{1,0:T(1,128)}, s32[1,64]{1,0:T(1,128)S(1)}, u32[]{:S(2)}, u32[]{:S(2)}) collective-permute-start(s32[1,64]{1,0:T(1,128)} %param.5), channel_id=1, source_target_pairs={{0,1},{1,2},{2,3},{3,4},{4,5},{5,6},{6,7},{7,8},{8,9},{9,10},{10,1... | collective-permute-start | bytes 776 | tf_op jit(solution)/shard_map/ppermute | solution.py:17
  15.6 26.0 %collective-permute-start.1 = (bf16[1,64,128,128]{3,2,1,0:T(8,128)(2,1)}, bf16[1,64,128,128]{3,2,1,0:T(8,128)(2,1)}, u32[]{:S(2)}, u32[]{:S(2)}) collective-permute-start(bf16[1,64,128,128]{3,2,1,0:T(8,128)(2,1)} %bitcast.7), channel_id=1, source_target_pairs={{1,0},{2,1},{3,2},{4,3},{5,4},{6,5},{7,6},{8,7},{9,8},{10,9},{11,1... | collective-permute-start | bytes 6291464 | tf_op jit(solution)/shard_map/ppermute | solution.py:17
  17.8 3.9 %copy-start.1 = (s32[1,64]{1,0:T(1,128)S(1)}, s32[1,64]{1,0:T(1,128)}, u32[]{:S(2)}) copy-start(s32[1,64]{1,0:T(1,128)} %param.5) | copy-start | bytes 772
  71.4 3.4 %copy-start = (f32[64,128,128]{2,1,0:T(8,128)S(1)}, f32[64,128,128]{2,1,0:T(8,128)}, u32[]{:S(2)}) copy-start(f32[64,128,128]{2,1,0:T(8,128)} %get-tuple-element.13) | copy-start | bytes 12582916
  76.6 6.0 %collective-permute-start.3 = (f32[1,3,128]{2,1,0:T(4,128)S(1)}, f32[1,3,128]{2,1,0:T(4,128)S(1)}, u32[]{:S(2)}, u32[]{:S(2)}) collective-permute-start(f32[1,3,128]{2,1,0:T(4,128)S(1)} %maximum_bitcast_fusion), channel_id=1, source_target_pairs={{0,1},{1,2},{2,3},{3,4},{4,5},{5,6},{6,7},{7,8},{8,9},{9,10},{10,1... | collective-permute-start | bytes 4616 | tf_op jit(solution)/shard_map/ppermute | solution.py:17
  82.7 4.6 %collective-permute-start.5 = (f32[1,2,128]{2,1,0:T(2,128)S(1)}, f32[1,2,128]{2,1,0:T(2,128)S(1)}, u32[]{:S(2)}, u32[]{:S(2)}) collective-permute-start(f32[1,2,128]{2,1,0:T(2,128)S(1)} %multiply_subtract_fusion.2), channel_id=1, source_target_pairs={{1,0},{2,1},{3,2},{4,3},{5,4},{6,5},{7,6},{8,7},{9,8},{10,9},{11,1... | collective-permute-start | bytes 3080 | tf_op jit(solution)/shard_map/ppermute | solution.py:28
  84.6 5.8 %collective-permute-start.6 = (f32[1,2,128]{2,1,0:T(2,128)S(1)}, f32[1,2,128]{2,1,0:T(2,128)S(1)}, u32[]{:S(2)}, u32[]{:S(2)}) collective-permute-start(f32[1,2,128]{2,1,0:T(2,128)S(1)} %multiply_subtract_fusion.2), channel_id=1, source_target_pairs={{0,1},{1,2},{2,3},{3,4},{4,5},{5,6},{6,7},{7,8},{8,9},{9,10},{10,1... | collective-permute-start | bytes 3080 | tf_op jit(solution)/shard_map/ppermute | solution.py:25
  90.6 4.5 %collective-permute-start.7 = (f32[1,2,128]{2,1,0:T(2,128)S(1)}, f32[1,2,128]{2,1,0:T(2,128)S(1)}, u32[]{:S(2)}, u32[]{:S(2)}) collective-permute-start(f32[1,2,128]{2,1,0:T(2,128)S(1)} %multiply_subtract_fusion.1), channel_id=1, source_target_pairs={{1,0},{2,1},{3,2},{4,3},{5,4},{6,5},{7,6},{8,7},{9,8},{10,9},{11,1... | collective-permute-start | bytes 3080 | tf_op jit(solution)/shard_map/ppermute | solution.py:28
  92.5 5.8 %collective-permute-start.8 = (f32[1,2,128]{2,1,0:T(2,128)S(1)}, f32[1,2,128]{2,1,0:T(2,128)S(1)}, u32[]{:S(2)}, u32[]{:S(2)}) collective-permute-start(f32[1,2,128]{2,1,0:T(2,128)S(1)} %multiply_subtract_fusion.1), channel_id=1, source_target_pairs={{0,1},{1,2},{2,3},{3,4},{4,5},{5,6},{6,7},{7,8},{8,9},{9,10},{10,1... | collective-permute-start | bytes 3080 | tf_op jit(solution)/shard_map/ppermute | solution.py:25
where the time goes:
time: 99.4 us; the launch traced here: 98.9 us
  matrix products  34.7 us (35%)
  waiting for transfers between devices  26 us (26%)
  starting transfers between devices  20.6 us (21%)
  local copies, waits for them, and re-layouts  8.1 us (8%)
  other arithmetic  7.92 us (8%)
  between operations  1.53 us (2%)
    dot_general x10, matrix products, left_mul(): jnp.einsum('kx,lxy->lky', dft_table, patch_block, preferred_element_type=...  21.7 us
    ppermute x3, waiting for transfers between devices, from_behind(): return lax.ppermute(block, axis, route)  19.6 us
    dot_general x6, matrix products, right_mul(): jnp.einsum('lxy,yk->lxk', patch_block, dft_table, preferred_element_type=...  12.8 us
    ppermute x3, starting transfers between devices, from_behind(): return lax.ppermute(block, axis, route)  7.32 us
    ppermute x3, starting transfers between devices, padded_2(): lax.ppermute(lax.slice_in_dim(block, block.shape[dim] - width, None, axis...  6.73 us
    ppermute x3, starting transfers between devices, padded_2(): lax.ppermute(lax.slice_in_dim(block, 0, width, axis=dim), axis, backward)  6.58 us
    ppermute x3, waiting for transfers between devices, padded_2(): lax.ppermute(lax.slice_in_dim(block, block.shape[dim] - width, None, axis...  6.34 us
    gather x1, local copies, waits for them, and re-layouts, on_device(): picked = own_patches[lower_list[0]]  4.36 us
  transfers between devices with their start and end apart: 9, of which 5 were waited for; matrix products, arithmetic and copies ran while one was open for 50% of the time, Pallas kernels for 0%

commit v1 on v0

v1 whole, which is shorter than its diff:
```python
import functools

import jax
import jax.numpy as jnp
import numpy as np
from jax import lax
from jax.experimental import pallas as pl
from jax.experimental.pallas import tpu as pltpu
from jax.sharding import PartitionSpec as P

GR = 8
SPRING = 0.25
STEP = 0.15
CHUNK = 8
EARLY = 2
HALO = 3
MESH = pl.DeviceIdType.MESH
F32 = jnp.float32
BF16 = jnp.bfloat16
HIGH = lax.Precision.HIGHEST


def dft_tables(length):
    index = np.arange(length)
    angle = (index[:, None] * index[None, :] % length) * (2.0 * np.pi / length)
    c = np.cos(angle).astype(np.float32)
    s = np.sin(angle).astype(np.float32)
    right = np.concatenate([c, s], axis=1)
    left = np.block([[c, -s], [-s, -c]])
    inner = np.block([[c, s], [-s, c]])
    last = np.concatenate([c, -s], axis=1)
    return tuple(jnp.asarray(t.astype(jnp.bfloat16)) for t in (right, left, inner, last))


def dot(a, b):
    return jnp.dot(a, b, preferred_element_type=F32)


def dot_nt(a, b):
    return lax.dot_general(a, b, (((1,), (1,)), ((), ())), precision=HIGH, preferred_element_type=F32)


def stacked(both, a, b, side):
    ra = both[a * side : (a + 1) * side]
    rb = both[b * side : (b + 1) * side]
    top = jnp.concatenate([ra[:, :side], rb[:, :side]], axis=1)
    low = jnp.concatenate([ra[:, side:], rb[:, side:]], axis=1)
    return jnp.concatenate([top, low], axis=0)


def spectra(images, right, left):
    side = images[0].shape[0]
    rows = jnp.concatenate(images, axis=0)
    both = dot(rows, right).astype(BF16)
    return [dot(left, stacked(both, 2 * i, 2 * i + 1, side)) for i in range(len(images) // 2)]


def lane_roll(x, shift):
    return pltpu.roll(x, shift % x.shape[-1], x.ndim - 1)


def kernel(
    n,
    right_ref,
    left_ref,
    inner_ref,
    last_ref,
    list_s,
    list_v,
    count_s,
    tissue_ref,
    patches_any,
    flow_ref,
    pos_ref,
    patches,
    far_list_v,
    far_list_s,
    outgoing,
    incoming,
    lower_spec,
    peak_ref,
    mass_ref,
    moment_ref,
    packet,
    halo,
    load_sem,
    smem_sem,
    list_sems,
    send_sems,
    recv_sems,
    halo_send,
    halo_recv,
):
    me = lax.axis_index("sec")
    total, side, _ = patches.shape
    slots = list_s.shape[1]
    chunks = slots // CHUNK
    offsets = [d for d in range(-HALO, HALO + 1) if d != 0]

    load = pltpu.make_async_copy(patches_any.at[0], patches, load_sem)
    load.start()

    halo[...] = jnp.zeros_like(halo)
    peak_ref[...] = jnp.zeros_like(peak_ref)
    mass_ref[...] = jnp.ones_like(mass_ref)
    moment_ref[...] = jnp.zeros_like(moment_ref)

    barrier = pltpu.get_barrier_semaphore()
    for d in offsets:

        @pl.when((me + d >= 0) & (me + d < n))
        def _():
            pl.semaphore_signal(barrier, inc=1, device_id={"sec": me + d}, device_id_type=MESH)

    pl.semaphore_wait(barrier, jnp.minimum(me, HALO) + jnp.minimum(n - 1 - me, HALO))

    list_copy = pltpu.make_async_remote_copy(
        src_ref=list_v,
        dst_ref=far_list_v,
        send_sem=list_sems.at[0],
        recv_sem=list_sems.at[1],
        device_id={"sec": me + 1},
        device_id_type=MESH,
    )

    @pl.when(me < n - 1)
    def _():
        list_copy.start()

    load.wait()

    def lower_group(g, carry):
        images = [patches[list_s[0, g * CHUNK + j]] for j in range(CHUNK)]
        for i, spec in enumerate(spectra(images, right_ref[...], left_ref[...])):
            lower_spec[g * (CHUNK // 2) + i] = spec.astype(BF16)
        return carry

    lax.fori_loop(0, EARLY, lower_group, 0)

    def patch_copy(c):
        return pltpu.make_async_remote_copy(
            src_ref=outgoing.at[pl.ds(c * CHUNK, CHUNK)],
            dst_ref=incoming.at[pl.ds(c * CHUNK, CHUNK)],
            send_sem=send_sems.at[c],
            recv_sem=recv_sems.at[c],
            device_id={"sec": me - 1},
            device_id_type=MESH,
        )

    @pl.when(me > 0)
    def _():
        list_copy.wait_recv()
        to_smem = pltpu.make_async_copy(far_list_v, far_list_s, smem_sem)
        to_smem.start()
        to_smem.wait()

        def gather(c):
            for j in range(CHUNK):
                outgoing[c * CHUNK + j] = patches[far_list_s[0, c * CHUNK + j]]

        gather(0)

        def send(c, carry):
            gather(c + 1)
            patch_copy(c).start()
            return carry

        lax.fori_loop(0, chunks - 1, send, 0)
        patch_copy(chunks - 1).start()

    lax.fori_loop(EARLY, chunks, lower_group, 0)

    half = side // 2
    row = lax.broadcasted_iota(jnp.int32, (side, 1), 0)
    row_lag = ((row + half) % side - half).astype(F32)
    scale = 64.0 / float(side * side * side * side)

    @pl.when(me < n - 1)
    def _():
        def upper_group(g, carry):
            patch_copy(g).wait_recv()
            images = [incoming[g * CHUNK + j] for j in range(CHUNK)]
            crosses = []
            for i, spec in enumerate(spectra(images, right_ref[...], left_ref[...])):
                ur = spec[:side].astype(BF16).astype(F32)
                ui = spec[side:].astype(BF16).astype(F32)
                low = lower_spec[g * (CHUNK // 2) + i].astype(F32)
                lr, li = low[:side], low[side:]
                cr = (lr * ur + li * ui).astype(BF16)
                ci = (lr * ui - li * ur).astype(BF16)
                crosses.append(jnp.concatenate([cr[:, :side], ci[:, :side]], axis=1))
                crosses.append(jnp.concatenate([cr[:, side:], ci[:, side:]], axis=1))
            inner = dot(jnp.concatenate(crosses, axis=0), inner_ref[...]).astype(BF16)
            peaks, masses, moments = [], [], []
            for i in range(CHUNK // 2):
                scores = dot(last_ref[...], stacked(inner, 2 * i, 2 * i + 1, side)) * scale
                peak = jnp.max(scores, axis=0, keepdims=True)
                e = jnp.exp(scores - peak)
                mass = jnp.sum(e, axis=0, keepdims=True)
                moment = jnp.sum(e * row_lag, axis=0, keepdims=True)
                for parts, value in ((peaks, peak), (masses, mass), (moments, moment)):
                    parts.append(value[:, :side])
                    parts.append(value[:, side:])
            at = pl.ds(pl.multiple_of(g * CHUNK, CHUNK), CHUNK)
            peak_ref[at, :] = jnp.concatenate(peaks, axis=0)
            mass_ref[at, :] = jnp.concatenate(masses, axis=0)
            moment_ref[at, :] = jnp.concatenate(moments, axis=0)
            return carry

        lax.fori_loop(0, chunks, upper_group, 0)

    peak = peak_ref[...]
    weight = jnp.exp(peak - jnp.max(peak, axis=1, keepdims=True))
    mass = mass_ref[...] * weight
    moment = moment_ref[...] * weight
    col = lax.broadcasted_iota(jnp.int32, (8, side), 1)
    sub = lax.broadcasted_iota(jnp.int32, (8, side), 0)
    col_lag = ((col + half) % side - half).astype(F32)
    probe = jnp.where(sub == 0, 1.0, jnp.where(sub == 1, col_lag, 0.0))
    sums = dot_nt(probe, mass)
    rows_num = dot_nt(probe, moment)
    mass_all = sums[0:1]
    live = lax.broadcasted_iota(jnp.int32, (1, slots), 1) < count_s[0]
    flow_rows = jnp.where(live, rows_num[0:1] / mass_all, 0.0)
    flow_cols = jnp.where(live, sums[1:2] / mass_all, 0.0)
    flow_ref[0] = jnp.concatenate([flow_rows, flow_cols], axis=0)
    which = lax.broadcasted_iota(jnp.int32, (total, slots), 0)
    onehot = (which == list_v[...]).astype(F32)
    stack = jnp.concatenate(
        [flow_rows, flow_cols, live.astype(F32), jnp.zeros((5, slots), F32)], axis=0
    )
    field = dot_nt(stack, onehot)
    sub_t = lax.broadcasted_iota(jnp.int32, (8, total), 0)
    packet[...] = jnp.where(sub_t == 3, tissue_ref[...].astype(F32), field)

    reach = [d for d in range(-HALO + 1, HALO + 1) if d != 0]

    def halo_copy(d):
        return pltpu.make_async_remote_copy(
            src_ref=packet,
            dst_ref=halo.at[HALO - d],
            send_sem=halo_send.at[HALO - d],
            recv_sem=halo_recv.at[HALO - d],
            device_id={"sec": me + d},
            device_id_type=MESH,
        )

    for d in reach:

        @pl.when((me + d >= 0) & (me + d < n))
        def _():
            halo_copy(d).start()

    for d in reach:

        @pl.when((me - d >= 0) & (me - d < n))
        def _():
            halo_copy(d).wait_recv()

    fields = {d: halo[HALO + d] for d in range(-HALO, HALO) if d != 0}
    fields[0] = packet[...]
    links = {d: jnp.broadcast_to(f[2:3], f.shape) for d, f in fields.items()}
    lane = lax.broadcasted_iota(jnp.int32, (8, total), 1)
    width = total // GR
    has_right = (lane % width) != width - 1
    has_below = lane < total - width

    def springs(d):
        tissue = jnp.broadcast_to(fields[d][3:4], (8, total))
        stiff = SPRING * (1.0 + 2.0 * tissue)
        across = jnp.where(has_right, 0.5 * (stiff + lane_roll(stiff, -1)), 0.0)
        along = jnp.where(has_below, 0.5 * (stiff + lane_roll(stiff, -width)), 0.0)
        return across, along

    def plane(u, spring):
        across, along = spring
        a = across * (lane_roll(u, -1) - u)
        b = along * (lane_roll(u, -width) - u)
        return (lane_roll(a, 1) - a) + (lane_roll(b, width) - b)

    spring = {d: springs(d) for d in (-1, 0, 1)}
    pull = {d: links[d] * fields[d] for d in fields}
    u1 = {d: -STEP * (pull[d] - pull[d - 1]) for d in range(-2, 3)}

    def relaxed(u, d):
        gap_here = u[d + 1] - u[d] - fields[d]
        gap_below = u[d] - u[d - 1] - fields[d - 1]
        force = plane(u[d], spring[d]) - links[d] * gap_here + links[d - 1] * gap_below
        return u[d] - STEP * force

    u2 = {d: relaxed(u1, d) for d in (-1, 0, 1)}
    pos_ref[0] = relaxed(u2, 0)[0:2]

    @pl.when(me < n - 1)
    def _():
        list_copy.wait_send()

    @pl.when(me > 0)
    def _():
        def drain(c, carry):
            patch_copy(c).wait_send()
            return carry

        lax.fori_loop(0, chunks, drain, 0)

    for d in reach:

        @pl.when((me + d >= 0) & (me + d < n))
        def _():
            halo_copy(d).wait_send()


def on_device(n, patches, pair_list, pair_count, tissue):
    _, total, side, _ = patches.shape
    slots = pair_list.shape[1]
    chunks = slots // CHUNK
    vmem = pl.BlockSpec(memory_space=pltpu.VMEM)
    smem = pl.BlockSpec(memory_space=pltpu.SMEM)
    dma = pltpu.SemaphoreType.DMA
    return pl.pallas_call(
        functools.partial(kernel, n),
        out_shape=(
            jax.ShapeDtypeStruct((1, 2, slots), F32),
            jax.ShapeDtypeStruct((1, 2, total), F32),
        ),
        in_specs=[vmem] * 4 + [smem, vmem, smem, vmem, pl.BlockSpec(memory_space=pl.ANY)],
        out_specs=(vmem, vmem),
        scratch_shapes=[
            pltpu.VMEM((total, side, side), BF16),
            pltpu.VMEM((1, slots), jnp.int32),
            pltpu.SMEM((1, slots), jnp.int32),
            pltpu.VMEM((slots, side, side), BF16),
            pltpu.VMEM((slots, side, side), BF16),
            pltpu.VMEM((slots // 2, 2 * side, 2 * side), BF16),
            pltpu.VMEM((slots, side), F32),
            pltpu.VMEM((slots, side), F32),
            pltpu.VMEM((slots, side), F32),
            pltpu.VMEM((8, total), F32),
            pltpu.VMEM((2 * HALO + 1, 8, total), F32),
            dma,
            dma,
            dma((2,)),
            dma((chunks,)),
            dma((chunks,)),
            dma((2 * HALO + 1,)),
            dma((2 * HALO + 1,)),
        ],
        compiler_params=pltpu.CompilerParams(
            collective_id=0, has_side_effects=True, vmem_limit_bytes=64_000_000
        ),
        name="section_match",
    )(*dft_tables(side), pair_list, pair_list, pair_count, tissue, patches)


def solution(mesh):
    return jax.shard_map(
        functools.partial(on_device, mesh.shape["sec"]),
        mesh=mesh,
        in_specs=(
            P(("group", "sec"), None, None, None),
            P(("group", "sec"), None),
            P(("group", "sec")),
            P(("group", "sec"), None),
        ),
        out_specs=(P(("group", "sec"), None, None), P(("group", "sec"), None, None)),
        check_vma=False,
    )
```

time: 99.4 us -> 40.9 us (0.41)
  the two profiles are of different devices: /device:TPU:24 before, /device:TPU:1 now
where the time goes in v1:
time: 40.9 us; the launch traced here: 40.8 us
  Pallas kernels  37 us (90%)
  local copies, waits for them, and re-layouts  2.44 us (6%)
  between operations  1.28 us (3%)
    pallas_call x1, Pallas kernels, on_device(): pl.pallas_call(functools.partial(kernel, n), out_shape=(jax.ShapeDtypeStr...  37 us
    unnamed x2, local copies, waits for them, and re-layouts  2.44 us

profile of v1, /device:TPU:1, one launch (start us, length us, event | category | flops | bytes accessed | tf_op | source)
XLA Modules:
  0.0 40.8 jit_solution(9254749891470036792)
XLA Ops:
  1.3 37.0 %section_match.1 = (f32[1,2,64]{2,1,0:T(2,128)}, f32[1,2,128]{2,1,0:T(2,128)}) custom-call(bf16[128,256]{1,0:T(8,128)(2,1)} %constant.8.clone.right_ref, bf16[256,256]{1,0:T(8,128)(2,1)} %constant.9.clone.left_ref, bf16[256,256]{1,0:T(8,128)(2,1)} %constant.10.clone.inner_ref, bf16[128,256]{1,0:T(8,128)(2,1)} %constant.11.clone.last_ref, s32[1,64]{1,0:T(1,128)} %list_v.1, ...), custom_call_target="tpu_custom_call" | custom-call | tf_op jit(solution)/shard_map/section_match/pallas_call | solution.py:320
  38.3 1.2 %copy.13 = f32[1,2,64]{2,1,0:T(2,128)} copy(f32[1,2,64]{2,1,0:T(2,128)} %get-tuple-element.4) | data formatting | bytes 1024
  39.5 1.2 %copy.14 = f32[1,2,128]{2,1,0:T(2,128)} copy(f32[1,2,128]{2,1,0:T(2,128)} %get-tuple-element.5) | data formatting | bytes 2048

commit v2 on v1

v2 whole, which is shorter than its diff:
```python
import functools

import jax
import jax.numpy as jnp
import numpy as np
from jax import lax
from jax.experimental import pallas as pl
from jax.experimental.pallas import tpu as pltpu
from jax.sharding import PartitionSpec as P

GR = 8
SPRING = 0.25
STEP = 0.15
CHUNK = 8
HALO = 3
MESH = pl.DeviceIdType.MESH
F32 = jnp.float32
BF16 = jnp.bfloat16
HIGH = lax.Precision.HIGHEST


def dft_tables(length):
    index = np.arange(length)
    angle = (index[:, None] * index[None, :] % length) * (2.0 * np.pi / length)
    c = np.cos(angle).astype(np.float32)
    s = np.sin(angle).astype(np.float32)
    right = np.concatenate([c, s], axis=1)
    left = np.block([[c, -s], [-s, -c]])
    inner = np.block([[c, s], [-s, c]])
    last = np.concatenate([c, -s], axis=1)
    return tuple(jnp.asarray(t.astype(jnp.bfloat16)) for t in (right, left, inner, last))


def dot(a, b):
    return jnp.dot(a, b, preferred_element_type=F32)


def dot_nt(a, b):
    return lax.dot_general(a, b, (((1,), (1,)), ((), ())), precision=HIGH, preferred_element_type=F32)


def stacked(both, a, b, side):
    ra = both[a * side : (a + 1) * side]
    rb = both[b * side : (b + 1) * side]
    top = jnp.concatenate([ra[:, :side], rb[:, :side]], axis=1)
    low = jnp.concatenate([ra[:, side:], rb[:, side:]], axis=1)
    return jnp.concatenate([top, low], axis=0)


def spectra(images, right, left):
    side = images[0].shape[0]
    rows = jnp.concatenate(images, axis=0)
    both = dot(rows, right).astype(BF16)
    return [dot(left, stacked(both, 2 * i, 2 * i + 1, side)) for i in range(len(images) // 2)]


def lane_roll(x, shift):
    return pltpu.roll(x, shift % x.shape[-1], x.ndim - 1)


def up_chunks(pair, n, chunks):
    odd = pair % 2
    across = n // 2 - 1
    k = pair // 2
    return odd * (chunks * (k + 1) // (across + 1)) + (1 - odd) * (chunks // 2)


def exchange(
    n,
    right_any,
    left_any,
    inner_any,
    last_any,
    list_any,
    count_s,
    tissue_any,
    patches_any,
    out_ref,
    patches,
    right_ref,
    left_ref,
    inner_ref,
    last_ref,
    list_v,
    list_s,
    tissue_v,
    note,
    far_note,
    far_s,
    outgoing,
    incoming,
    own_spec,
    peak_ref,
    mass_ref,
    moment_ref,
    packet,
    halo,
    load_sems,
    smem_sem,
    list_sems,
    send_sems,
    recv_sems,
    halo_send,
    halo_recv,
):
    me = lax.axis_index("sec")
    total, side, _ = patches.shape
    slots = list_v.shape[1]
    chunks = slots // CHUNK
    offsets = [d for d in range(-HALO, HALO + 1) if d != 0]

    loads = [
        pltpu.make_async_copy(source, target, load_sems.at[i])
        for i, (source, target) in enumerate(
            (
                (list_any, list_v),
                (list_any, list_s),
                (patches_any.at[0], patches),
                (right_any, right_ref),
                (left_any, left_ref),
                (inner_any, inner_ref),
                (last_any, last_ref),
                (tissue_any, tissue_v),
            )
        )
    ]
    for load in loads:
        load.start()

    halo[...] = jnp.zeros_like(halo)
    far_note[...] = jnp.zeros_like(far_note)

    barrier = pltpu.get_barrier_semaphore()
    for d in offsets:

        @pl.when((me + d >= 0) & (me + d < n))
        def _():
            pl.semaphore_signal(barrier, inc=1, device_id={"sec": me + d}, device_id_type=MESH)

    peak_ref[...] = jnp.zeros_like(peak_ref)
    mass_ref[...] = jnp.ones_like(mass_ref)
    moment_ref[...] = jnp.zeros_like(moment_ref)
    for load in loads[:2]:
        load.wait()
    count = count_s[0]
    note[...] = jnp.concatenate([list_v[...], jnp.full((1, slots), count, jnp.int32)], axis=0)

    has_up = jnp.minimum(n - 1 - me, 1)
    has_down = jnp.minimum(me, 1)
    my_up = up_chunks(me, n, chunks)
    far_up = up_chunks(me - 1, n, chunks)

    pl.semaphore_wait(barrier, jnp.minimum(me, HALO) + jnp.minimum(n - 1 - me, HALO))

    list_copy = pltpu.make_async_remote_copy(
        src_ref=note,
        dst_ref=far_note,
        send_sem=list_sems.at[0],
        recv_sem=list_sems.at[1],
        device_id={"sec": me + 1},
        device_id_type=MESH,
    )

    @pl.when(me < n - 1)
    def _():
        list_copy.start()

    loads[2].wait()

    def patch_copy(q, to):
        return pltpu.make_async_remote_copy(
            src_ref=outgoing.at[pl.ds(q * CHUNK, CHUNK)],
            dst_ref=incoming.at[pl.ds(q * CHUNK, CHUNK)],
            send_sem=send_sems.at[q],
            recv_sem=recv_sems.at[q],
            device_id={"sec": to},
            device_id_type=MESH,
        )

    def send_up(c, carry):
        for j in range(CHUNK):
            outgoing[c * CHUNK + j] = patches[list_s[0, c * CHUNK + j]]
        patch_copy(c, me + 1).start()
        return carry

    lax.fori_loop(0, has_up * my_up, send_up, 0)
    for load in loads[3:]:
        load.wait()

    def own_group(q, carry):
        images = []
        for j in range(CHUNK):
            far = far_s[0, jnp.minimum(q, chunks - 1) * CHUNK + j]
            near = list_s[0, jnp.maximum(q - chunks, 0) * CHUNK + j]
            images.append(patches[jnp.where(q < chunks, far, near)])
        for i, spec in enumerate(spectra(images, right_ref[...], left_ref[...])):
            own_spec[q * (CHUNK // 2) + i] = spec.astype(BF16)
        return carry

    @pl.when(me > 0)
    def _():
        list_copy.wait_recv()

    to_smem = pltpu.make_async_copy(far_note, far_s, smem_sem)
    to_smem.start()
    to_smem.wait()

    def send_down(c, carry):
        for j in range(CHUNK):
            outgoing[slots + c * CHUNK + j] = patches[far_s[0, c * CHUNK + j]]
        patch_copy(chunks + c, me - 1).start()
        return carry

    lax.fori_loop(far_up, far_up + has_down * (chunks - far_up), send_down, 0)
    lax.fori_loop(chunks + my_up, chunks + my_up + has_up * (chunks - my_up), own_group, 0)
    lax.fori_loop(0, has_down * far_up, own_group, 0)

    half = side // 2
    row = lax.broadcasted_iota(jnp.int32, (side, 1), 0)
    row_lag = ((row + half) % side - half).astype(F32)
    scale = 64.0 / float(side * side * side * side)

    def match_group(t, carry):
        start_a, count_a, start_b = carry
        q = jnp.where(t < count_a, start_a + t, start_b + t - count_a)
        patch_copy(q, me).wait_recv()
        sign = jnp.where(q < chunks, -1.0, 1.0).astype(F32)
        images = [incoming[q * CHUNK + j] for j in range(CHUNK)]
        crosses = []
        for i, spec in enumerate(spectra(images, right_ref[...], left_ref[...])):
            ar = spec[:side].astype(BF16).astype(F32)
            ai = spec[side:].astype(BF16).astype(F32)
            own = own_spec[q * (CHUNK // 2) + i].astype(F32)
            br, bi = own[:side], own[side:]
            cr = (br * ar + bi * ai).astype(BF16)
            ci = ((br * ai - bi * ar) * sign).astype(BF16)
            crosses.append(jnp.concatenate([cr[:, :side], ci[:, :side]], axis=1))
            crosses.append(jnp.concatenate([cr[:, side:], ci[:, side:]], axis=1))
        inner = dot(jnp.concatenate(crosses, axis=0), inner_ref[...]).astype(BF16)
        peaks, masses, moments = [], [], []
        for i in range(CHUNK // 2):
            scores = dot(last_ref[...], stacked(inner, 2 * i, 2 * i + 1, side)) * scale
            peak = jnp.max(scores, axis=0, keepdims=True)
            e = jnp.exp(scores - peak)
            mass = jnp.sum(e, axis=0, keepdims=True)
            moment = jnp.sum(e * row_lag, axis=0, keepdims=True)
            for parts, value in ((peaks, peak), (masses, mass), (moments, moment)):
                parts.append(value[:, :side])
                parts.append(value[:, side:])
        at = pl.ds(pl.multiple_of(q * CHUNK, CHUNK), CHUNK)
        peak_ref[at, :] = jnp.concatenate(peaks, axis=0)
        mass_ref[at, :] = jnp.concatenate(masses, axis=0)
        moment_ref[at, :] = jnp.concatenate(moments, axis=0)
        return carry

    n_far = has_down * far_up
    n_near = has_up * (chunks - my_up)
    odd = me % 2
    start_a = (1 - odd) * (chunks + my_up)
    start_b = odd * (chunks + my_up)
    count_a = odd * n_far + (1 - odd) * n_near
    lax.fori_loop(0, n_far + n_near, match_group, (start_a, count_a, start_b))

    peak = peak_ref[...]
    weight = jnp.exp(peak - jnp.max(peak, axis=1, keepdims=True))
    mass = mass_ref[...] * weight
    moment = moment_ref[...] * weight
    col = lax.broadcasted_iota(jnp.int32, (8, side), 1)
    sub = lax.broadcasted_iota(jnp.int32, (8, side), 0)
    col_lag = ((col + half) % side - half).astype(F32)
    axes = jnp.where(sub == 0, 1.0, jnp.where(sub == 1, col_lag, 0.0))
    sums = dot_nt(axes, mass)
    rows_num = dot_nt(axes, moment)
    mass_all = sums[0:1]
    place = lax.broadcasted_iota(jnp.int32, (1, 2 * slots), 1)
    is_far = place < slots
    far = far_note[...]
    counts = jnp.concatenate([far[1:2], jnp.full((1, slots), count, jnp.int32)], axis=1)
    lists = jnp.concatenate([far[0:1], list_v[...]], axis=1)
    slot = jnp.where(is_far, place, place - slots)
    first = jnp.where(is_far, 0, (chunks - n_near) * CHUNK)
    stop = jnp.minimum(jnp.where(is_far, n_far * CHUNK, slots), counts)
    live = (slot >= first) & (slot < stop)
    flow_rows = jnp.where(live, rows_num[0:1] / mass_all, 0.0)
    flow_cols = jnp.where(live, sums[1:2] / mass_all, 0.0)
    which = lax.broadcasted_iota(jnp.int32, (total, 2 * slots), 0)
    onehot = (which == lists).astype(F32)
    one_pair = jnp.concatenate(
        [flow_rows, flow_cols, live.astype(F32), jnp.zeros((5, 2 * slots), F32)], axis=0
    )
    both = jnp.concatenate(
        [jnp.where(is_far, one_pair, 0.0), jnp.where(is_far, 0.0, one_pair)], axis=0
    )
    field = dot_nt(both, onehot)
    packet[0:3] = field[0:3]
    packet[3:4] = tissue_v[...].astype(F32)
    packet[4:8] = field[4:8]
    packet[8:16] = field[8:16]
    packet[4:5, 0 : 2 * slots] = flow_rows
    packet[5:6, 0 : 2 * slots] = flow_cols

    def halo_copy(d):
        return pltpu.make_async_remote_copy(
            src_ref=packet,
            dst_ref=halo.at[HALO - d],
            send_sem=halo_send.at[HALO - d],
            recv_sem=halo_recv.at[HALO - d],
            device_id={"sec": me + d},
            device_id_type=MESH,
        )

    for d in offsets:

        @pl.when((me + d >= 0) & (me + d < n))
        def _():
            halo_copy(d).start()

    @pl.when(me < n - 1)
    def _():
        list_copy.wait_send()

    def drain_up(c, carry):
        patch_copy(c, me + 1).wait_send()
        return carry

    lax.fori_loop(0, has_up * my_up, drain_up, 0)

    def drain_down(c, carry):
        patch_copy(chunks + c, me - 1).wait_send()
        return carry

    lax.fori_loop(far_up, far_up + has_down * (chunks - far_up), drain_down, 0)
    for d in offsets:

        @pl.when((me - d >= 0) & (me - d < n))
        def _():
            halo_copy(d).wait_recv()

    for d in offsets:
        out_ref[HALO + d] = halo[HALO + d]
    out_ref[HALO] = packet[...]
    for d in offsets:

        @pl.when((me + d >= 0) & (me + d < n))
        def _():
            halo_copy(d).wait_send()


def relax(halo, flow_ref, pos_ref):
    total = halo.shape[-1]
    slots = flow_ref.shape[-1]
    near, above = halo[HALO], halo[HALO + 1]
    flow_ref[0] = near[4:6, slots : 2 * slots] + above[4:6, 0:slots]
    fields = {d: halo[HALO + d][8:16] + halo[HALO + d + 1][0:8] for d in range(-HALO, HALO)}
    links = {d: jnp.broadcast_to(f[2:3], f.shape) for d, f in fields.items()}
    lane = lax.broadcasted_iota(jnp.int32, (8, total), 1)
    width = total // GR
    has_right = (lane % width) != width - 1
    has_below = lane < total - width

    def springs(d):
        tissue = jnp.broadcast_to(halo[HALO + d][3:4], (8, total))
        stiff = SPRING * (1.0 + 2.0 * tissue)
        across = jnp.where(has_right, 0.5 * (stiff + lane_roll(stiff, -1)), 0.0)
        along = jnp.where(has_below, 0.5 * (stiff + lane_roll(stiff, -width)), 0.0)
        return across, along

    def plane(u, spring):
        across, along = spring
        a = across * (lane_roll(u, -1) - u)
        b = along * (lane_roll(u, -width) - u)
        return (lane_roll(a, 1) - a) + (lane_roll(b, width) - b)

    spring = {d: springs(d) for d in (-1, 0, 1)}
    pull = {d: links[d] * fields[d] for d in fields}
    u1 = {d: -STEP * (pull[d] - pull[d - 1]) for d in range(-2, 3)}

    def relaxed(u, d):
        gap_here = u[d + 1] - u[d] - fields[d]
        gap_below = u[d] - u[d - 1] - fields[d - 1]
        force = plane(u[d], spring[d]) - links[d] * gap_here + links[d - 1] * gap_below
        return u[d] - STEP * force

    u2 = {d: relaxed(u1, d) for d in (-1, 0, 1)}
    pos_ref[0] = relaxed(u2, 0)[0:2]


def on_device(n, patches, pair_list, pair_count, tissue):
    _, total, side, _ = patches.shape
    slots = pair_list.shape[1]
    chunks = slots // CHUNK
    vmem = pl.BlockSpec(memory_space=pltpu.VMEM)
    any_space = pl.BlockSpec(memory_space=pl.ANY)
    dma = pltpu.SemaphoreType.DMA
    halo = pl.pallas_call(
        functools.partial(exchange, n),
        out_shape=jax.ShapeDtypeStruct((2 * HALO + 1, 16, total), F32),
        in_specs=[any_space] * 5 + [pl.BlockSpec(memory_space=pltpu.SMEM)] + [any_space] * 2,
        out_specs=vmem,
        scratch_shapes=[
            pltpu.VMEM((total, side, side), BF16),
            pltpu.VMEM((side, 2 * side), BF16),
            pltpu.VMEM((2 * side, 2 * side), BF16),
            pltpu.VMEM((2 * side, 2 * side), BF16),
            pltpu.VMEM((side, 2 * side), BF16),
            pltpu.VMEM((1, slots), jnp.int32),
            pltpu.SMEM((1, slots), jnp.int32),
            pltpu.VMEM((1, total), jnp.int32),
            pltpu.VMEM((2, slots), jnp.int32),
            pltpu.VMEM((2, slots), jnp.int32),
            pltpu.SMEM((2, slots), jnp.int32),
            pltpu.VMEM((2 * slots, side, side), BF16),
            pltpu.VMEM((2 * slots, side, side), BF16),
            pltpu.VMEM((slots, 2 * side, 2 * side), BF16),
            pltpu.VMEM((2 * slots, side), F32),
            pltpu.VMEM((2 * slots, side), F32),
            pltpu.VMEM((2 * slots, side), F32),
            pltpu.VMEM((16, total), F32),
            pltpu.VMEM((2 * HALO + 1, 16, total), F32),
            dma((8,)),
            dma,
            dma((2,)),
            dma((2 * chunks,)),
            dma((2 * chunks,)),
            dma((2 * HALO + 1,)),
            dma((2 * HALO + 1,)),
        ],
        compiler_params=pltpu.CompilerParams(
            collective_id=0, has_side_effects=True, vmem_limit_bytes=64_000_000
        ),
        name="exchange",
    )(*dft_tables(side), pair_list, pair_count, tissue, patches)
    return pl.pallas_call(
        relax,
        out_shape=(
            jax.ShapeDtypeStruct((1, 2, slots), F32),
            jax.ShapeDtypeStruct((1, 2, total), F32),
        ),
        in_specs=[vmem],
        out_specs=(vmem, vmem),
        name="relax",
    )(halo)


def solution(mesh):
    return jax.shard_map(
        functools.partial(on_device, mesh.shape["sec"]),
        mesh=mesh,
        in_specs=(
            P(("group", "sec"), None, None, None),
            P(("group", "sec"), None),
            P(("group", "sec")),
            P(("group", "sec"), None),
        ),
        out_specs=(P(("group", "sec"), None, None), P(("group", "sec"), None, None)),
        check_vma=False,
    )
```

time: 40.9 us -> 34.5 us (0.84)
  Pallas kernels: 37 us -> 32.7 us
  local copies, waits for them, and re-layouts: 2.44 us -> 0 us
    pallas_call x1 -> x2, Pallas kernels: 37 us -> 32.7 us  [the longest x1 31.1 us: on_device(): pl.pallas_call(functools.partial(exchange, n), out_shape=jax.ShapeDtypeSt...]
    unnamed x2 -> x0, local copies, waits for them, and re-layouts: 2.44 us -> none
where the time goes in v2:
time: 34.5 us; the launch traced here: 34 us
  Pallas kernels  32.7 us (95%)
  between operations  1.28 us (4%)
    pallas_call x1, Pallas kernels, on_device(): pl.pallas_call(functools.partial(exchange, n), out_shape=jax.ShapeDtypeSt...  31.1 us
    pallas_call x1, Pallas kernels, on_device(): pl.pallas_call(relax, out_shape=(jax.ShapeDtypeStruct((1, 2, slots), F32)...  1.68 us

profile of v2, /device:TPU:1, one launch (start us, length us, event | category | flops | bytes accessed | tf_op | source)
XLA Modules:
  0.0 34.0 jit_solution(6821994718288794093)
XLA Ops:
  1.3 31.1 %exchange.1.halo = f32[7,16,128]{2,1,0:T(8,128)} custom-call(bf16[128,256]{1,0:T(8,128)(2,1)} %constant.8.clone.right_any, bf16[256,256]{1,0:T(8,128)(2,1)} %constant.9.clone.left_any, bf16[256,256]{1,0:T(8,128)(2,1)} %constant.10.clone.inner_any, bf16[128,256]{1,0:T(8,128)(2,1)} %constant.11.clone.last_any, s32[1,64]{1,0:T(1,128)} %list_any.1, ...), custom_call_target="tpu_custom_call" | custom-call | tf_op jit(solution)/shard_map/exchange/pallas_call | solution.py:395
  32.3 1.7 %relax.1 = (f32[1,2,64]{2,1,0:T(2,128)}, f32[1,2,128]{2,1,0:T(2,128)}) custom-call(f32[7,16,128]{2,1,0:T(8,128)} %exchange.1.halo), custom_call_target="tpu_custom_call" | custom-call | tf_op jit(solution)/shard_map/relax/pallas_call | solution.py:433

commit v3 on v2

--- a/solution.py
+++ b/solution.py
@@ -16,7 +16,6 @@
 MESH = pl.DeviceIdType.MESH
 F32 = jnp.float32
 BF16 = jnp.bfloat16
-HIGH = lax.Precision.HIGHEST
 
 
 def dft_tables(length):
@@ -36,7 +35,14 @@
 
 
 def dot_nt(a, b):
-    return lax.dot_general(a, b, (((1,), (1,)), ((), ())), precision=HIGH, preferred_element_type=F32)
+    return lax.dot_general(a, b, (((1,), (1,)), ((), ())), preferred_element_type=F32)
+
+
+def split3(x):
+    top = x.astype(BF16)
+    rest = x - top.astype(F32)
+    mid = rest.astype(BF16)
+    return top, mid, (rest - mid.astype(F32)).astype(BF16)
 
 
 def stacked(both, a, b, side):
@@ -59,10 +65,7 @@
 
 
 def up_chunks(pair, n, chunks):
-    odd = pair % 2
-    across = n // 2 - 1
-    k = pair // 2
-    return odd * (chunks * (k + 1) // (across + 1)) + (1 - odd) * (chunks // 2)
+    return chunks * ((pair + 1) // 2) // (n // 2)
 
 
 def exchange(
@@ -269,8 +272,11 @@
     sub = lax.broadcasted_iota(jnp.int32, (8, side), 0)
     col_lag = ((col + half) % side - half).astype(F32)
     axes = jnp.where(sub == 0, 1.0, jnp.where(sub == 1, col_lag, 0.0))
-    sums = dot_nt(axes, mass)
-    rows_num = dot_nt(axes, moment)
+    thirds = jnp.concatenate(split3(jnp.concatenate([mass, moment], axis=0)), axis=0)
+    triple = dot_nt(axes.astype(BF16), thirds)
+    span = 4 * slots
+    joined = triple[:, 0:span] + triple[:, span : 2 * span] + triple[:, 2 * span :]
+    sums, rows_num = joined[:, 0 : 2 * slots], joined[:, 2 * slots :]
     mass_all = sums[0:1]
     place = lax.broadcasted_iota(jnp.int32, (1, 2 * slots), 1)
     is_far = place < slots
@@ -284,14 +290,15 @@
     flow_rows = jnp.where(live, rows_num[0:1] / mass_all, 0.0)
     flow_cols = jnp.where(live, sums[1:2] / mass_all, 0.0)
     which = lax.broadcasted_iota(jnp.int32, (total, 2 * slots), 0)
-    onehot = (which == lists).astype(F32)
+    onehot = (which == lists).astype(F32).astype(BF16)
     one_pair = jnp.concatenate(
         [flow_rows, flow_cols, live.astype(F32), jnp.zeros((5, 2 * slots), F32)], axis=0
     )
     both = jnp.concatenate(
         [jnp.where(is_far, one_pair, 0.0), jnp.where(is_far, 0.0, one_pair)], axis=0
     )
-    field = dot_nt(both, onehot)
+    triple = dot_nt(jnp.concatenate(split3(both), axis=0), onehot)
+    field = triple[0:16] + triple[16:32] + triple[32:48]
     packet[0:3] = field[0:3]
     packet[3:4] = tissue_v[...].astype(F32)
     packet[4:8] = field[4:8]

time: 34.5 us -> 34.1 us (0.988)
    pallas_call x1, Pallas kernels: 31.1 us -> 30.7 us  [on_device(): pl.pallas_call(functools.partial(exchange, n), out_shape=jax.ShapeDtypeSt...]
where the time goes in v3:
time: 34.1 us; the launch traced here: 33.6 us
  Pallas kernels  32.4 us (95%)
  between operations  1.28 us (4%)
    pallas_call x1, Pallas kernels, on_device(): pl.pallas_call(functools.partial(exchange, n), out_shape=jax.ShapeDtypeSt...  30.7 us
    pallas_call x1, Pallas kernels, on_device(): pl.pallas_call(relax, out_shape=(jax.ShapeDtypeStruct((1, 2, slots), F32)...  1.68 us

profile of v3, /device:TPU:1, one launch (start us, length us, event | category | flops | bytes accessed | tf_op | source)
XLA Modules:
  0.0 33.6 jit_solution(3844641943604886923)
XLA Ops:
  1.3 30.7 %exchange.1.halo = f32[7,16,128]{2,1,0:T(8,128)} custom-call(bf16[128,256]{1,0:T(8,128)(2,1)} %constant.8.clone.right_any, bf16[256,256]{1,0:T(8,128)(2,1)} %constant.9.clone.left_any, bf16[256,256]{1,0:T(8,128)(2,1)} %constant.10.clone.inner_any, bf16[128,256]{1,0:T(8,128)(2,1)} %constant.11.clone.last_any, s32[1,64]{1,0:T(1,128)} %list_any.1, ...), custom_call_target="tpu_custom_call" | custom-call | tf_op jit(solution)/shard_map/exchange/pallas_call | solution.py:402
  32.0 1.7 %relax.1 = (f32[1,2,64]{2,1,0:T(2,128)}, f32[1,2,128]{2,1,0:T(2,128)}) custom-call(f32[7,16,128]{2,1,0:T(8,128)} %exchange.1.halo), custom_call_target="tpu_custom_call" | custom-call | tf_op jit(solution)/shard_map/relax/pallas_call | solution.py:440

commit v4 on v3

--- a/solution.py
+++ b/solution.py
@@ -110,7 +110,7 @@
     total, side, _ = patches.shape
     slots = list_v.shape[1]
     chunks = slots // CHUNK
-    offsets = [d for d in range(-HALO, HALO + 1) if d != 0]
+    offsets = [d * sign for d in range(HALO, 0, -1) for sign in (1, -1)]
 
     loads = [
         pltpu.make_async_copy(source, target, load_sems.at[i])
@@ -140,9 +140,6 @@
         def _():
             pl.semaphore_signal(barrier, inc=1, device_id={"sec": me + d}, device_id_type=MESH)
 
-    peak_ref[...] = jnp.zeros_like(peak_ref)
-    mass_ref[...] = jnp.ones_like(mass_ref)
-    moment_ref[...] = jnp.zeros_like(moment_ref)
     for load in loads[:2]:
         load.wait()
     count = count_s[0]
@@ -187,6 +184,9 @@
         return carry
 
     lax.fori_loop(0, has_up * my_up, send_up, 0)
+    peak_ref[...] = jnp.zeros_like(peak_ref)
+    mass_ref[...] = jnp.ones_like(mass_ref)
+    moment_ref[...] = jnp.zeros_like(moment_ref)
     for load in loads[3:]:
         load.wait()
 
@@ -322,6 +322,12 @@
         def _():
             halo_copy(d).start()
 
+    for d in offsets:
+
+        @pl.when((me - d >= 0) & (me - d < n))
+        def _():
+            halo_copy(d).wait_recv()
+
     @pl.when(me < n - 1)
     def _():
         list_copy.wait_send()
@@ -337,12 +343,6 @@
         return carry
 
     lax.fori_loop(far_up, far_up + has_down * (chunks - far_up), drain_down, 0)
-    for d in offsets:
-
-        @pl.when((me - d >= 0) & (me - d < n))
-        def _():
-            halo_copy(d).wait_recv()
-
     for d in offsets:
         out_ref[HALO + d] = halo[HALO + d]
     out_ref[HALO] = packet[...]

time: 34.1 us -> 34.1 us (level)
  no operation moved by 1% of the time
where the time goes in v4:
time: 34.1 us; the launch traced here: 33.7 us
  Pallas kernels  32.4 us (95%)
  between operations  1.28 us (4%)
    pallas_call x1, Pallas kernels, on_device(): pl.pallas_call(functools.partial(exchange, n), out_shape=jax.ShapeDtypeSt...  30.7 us
    pallas_call x1, Pallas kernels, on_device(): pl.pallas_call(relax, out_shape=(jax.ShapeDtypeStruct((1, 2, slots), F32)...  1.68 us

profile of v4, /device:TPU:1, one launch (start us, length us, event | category | flops | bytes accessed | tf_op | source)
XLA Modules:
  0.0 33.7 jit_solution(10784084652054032178)
XLA Ops:
  1.3 30.7 %exchange.1.halo = f32[7,16,128]{2,1,0:T(8,128)} custom-call(bf16[128,256]{1,0:T(8,128)(2,1)} %constant.8.clone.right_any, bf16[256,256]{1,0:T(8,128)(2,1)} %constant.9.clone.left_any, bf16[256,256]{1,0:T(8,128)(2,1)} %constant.10.clone.inner_any, bf16[128,256]{1,0:T(8,128)(2,1)} %constant.11.clone.last_any, s32[1,64]{1,0:T(1,128)} %list_any.1, ...), custom_call_target="tpu_custom_call" | custom-call | tf_op jit(solution)/shard_map/exchange/pallas_call | solution.py:402
  32.0 1.7 %relax.1 = (f32[1,2,64]{2,1,0:T(2,128)}, f32[1,2,128]{2,1,0:T(2,128)}) custom-call(f32[7,16,128]{2,1,0:T(8,128)} %exchange.1.halo), custom_call_target="tpu_custom_call" | custom-call | tf_op jit(solution)/shard_map/relax/pallas_call | solution.py:440
